TPU v7x, 32 devices: a whole 2x2x4 slice. The times are simulated.
32 devices in a mesh: il: 16 (over z, y, core), xl: 2 (over x).
Axes of the slice: x: 2, y: 2, z: 4, core: 2. Of those that a mesh axis runs over, the one named last changes fastest.
Arguments:
- solution: float32 [64, 128, 512], P('il', 'xl'), may hold values from -6 to 6
- residual: float32 [64, 128, 512], P('il', 'xl'), may hold values from -30 to 30
- direction: float32 [64, 128, 512], P('il', 'xl'), may hold values from -30 to 30
- slope_il: float32 [64, 128, 512], P('il', 'xl'), may hold values from -1.5 to 1.5
- slope_xl: float32 [64, 128, 512], P('il', 'xl'), may hold values from -1.5 to 1.5
- weights: float32 [64, 128, 512], P('il', 'xl'), may hold values from 0.2 to 1
Outputs:
- new_solution: float32 [64, 128, 512], P('il', 'xl')
- new_residual: float32 [64, 128, 512], P('il', 'xl')
- new_direction: float32 [64, 128, 512], P('il', 'xl')
All inputs are finite; a program needn't handle non-finite values.
Results may differ from a plain program's by a relative error of at most 0.00002.
Values sent between devices are 32-bit elements; how exact they have to be, the bound alone decides.
No kernel may reach another device: no remote copies, remote signals or barrier semaphores. Data moves between devices by JAX's collectives and lax.ppermute only.
A program may use at most 64 MiB of HBM per device.

v0:
```python
import jax
import jax.numpy as jnp
from jax import lax
from jax.sharding import PartitionSpec as P

damping = 0.3


def padded_2(value, sides, width):
    for axis, dim in sides:
        size, length = (lax.axis_size(axis), value.shape[dim])
        up = [(i, (i + 1) % size) for i in range(size - 1)]
        down = [(j, i) for i, j in up]
        last = lax.slice_in_dim(value, length - width, length, axis=dim)
        first = lax.slice_in_dim(value, 0, width, axis=dim)
        before = lax.ppermute(last, axis, up)
        after = lax.ppermute(first, axis, down)
        value = jnp.concatenate([before, value, after], axis=dim)
    return value


def shifted(value, axis, by):
    length = lax.axis_size(axis)
    pairs = [(i, i + by) for i in range(length) if 0 <= i + by < length]
    return lax.ppermute(value, axis, pairs)


def time_diff(field):
    padded = jnp.pad(field, ((0, 0), (0, 0), (1, 1)))
    return 0.5 * (padded[:, :, 2:] - padded[:, :, :-2])


def normal_apply(direction, slope_il, slope_xl, weights):
    il_rows = direction.shape[0]
    xl_rows = direction.shape[1]
    total_il = il_rows * lax.axis_size("il")
    total_xl = xl_rows * lax.axis_size("xl")
    start_il = lax.axis_index("il") * il_rows
    start_xl = lax.axis_index("xl") * xl_rows
    field = padded_2(direction, (("il", 0), ("xl", 1)), 1)
    coef_il = shifted(jnp.stack([slope_il[-1:], weights[-1:]]), "il", 1)
    coef_xl = shifted(jnp.stack([slope_xl[:, -1:], weights[:, -1:]]), "xl", 1)
    current = field[:-1, 1:-1]
    slope_rows = jnp.concatenate([coef_il[0], slope_il], 0)
    weight_rows = jnp.concatenate([coef_il[1], weights], 0)
    global_il = start_il - 1 + jnp.arange(il_rows + 1)
    keep_il = (global_il < total_il - 1)[:, None, None]
    flux_il = jnp.where(
        keep_il,
        weight_rows * weight_rows * (field[1:, 1:-1] - current - slope_rows * time_diff(current)),
        0.0,
    )
    current = field[1:-1, :-1]
    slope_cols = jnp.concatenate([coef_xl[0], slope_xl], 1)
    weight_cols = jnp.concatenate([coef_xl[1], weights], 1)
    global_xl = start_xl - 1 + jnp.arange(xl_rows + 1)
    keep_xl = (global_xl < total_xl - 1)[None, :, None]
    flux_xl = jnp.where(
        keep_xl,
        weight_cols * weight_cols * (field[1:-1, 1:] - current - slope_cols * time_diff(current)),
        0.0,
    )
    term_il = flux_il[:-1] - flux_il[1:] + time_diff(slope_il * flux_il[1:])
    term_xl = flux_xl[:, :-1] - flux_xl[:, 1:] + time_diff(slope_xl * flux_xl[:, 1:])
    return term_il + term_xl + damping * direction


def body(solution, residual, direction, slope_il, slope_xl, weights):
    image = normal_apply(direction, slope_il, slope_xl, weights)
    norm_old, along, cross_term, image_norm = lax.psum(
        (
            jnp.sum(residual * residual),
            jnp.sum(direction * image),
            jnp.sum(residual * image),
            jnp.sum(image * image),
        ),
        ("il", "xl"),
    )
    alpha = norm_old / along
    new_residual = residual - alpha * image
    norm_new = norm_old - 2.0 * alpha * cross_term + alpha * alpha * image_norm
    new_solution = solution + alpha * direction
    new_direction = new_residual + norm_new / norm_old * direction
    return (new_solution, new_residual, new_direction)


def solution(mesh):
    placed = (
        P("il", "xl", None),
        P("il", "xl", None),
        P("il", "xl", None),
        P("il", "xl", None),
        P("il", "xl", None),
        P("il", "xl", None),
    )
    return jax.shard_map(
        body,
        mesh=mesh,
        in_specs=placed,
        out_specs=(P("il", "xl", None), P("il", "xl", None), P("il", "xl", None)),
        check_vma=False,
    )
```

profile of v0, /device:TPU:0, one launch (start us, length us, event | category | flops | bytes accessed | tf_op | source)
XLA Modules:
  0.0 73.8 jit_solution(13311208214205433469)
XLA Ops:
  0.6 1.0 %fusion.23 = (f32[1,64,512]{2,1,0:T(8,128)S(1)}, f32[1,64,512]{2,1,0:T(8,128)S(1)}) fusion(f32[4,64,512]{2,1,0:T(8,128)} %param.8), kind=kLoop, calls=%fused_computation.63 | loop fusion | bytes 524288 | tf_op jit(solution)/shard_map/slice | solution.py:15
  1.7 2.4 %collective-permute-start.2 = (f32[1,64,512]{2,1,0:T(8,128)S(1)}, f32[1,64,512]{2,1,0:T(8,128)S(1)}, u32[]{:S(2)}, u32[]{:S(2)}) collective-permute-start(f32[1,64,512]{2,1,0:T(8,128)S(1)} %get-tuple-element.20), channel_id=1, source_target_pairs={{0,2},{2,4},{4,6},{6,8},{8,10},{10,12},{12,14},{14,16},{16,18},{18... | collective-permute-start | bytes 393224 | tf_op jit(solution)/shard_map/ppermute | solution.py:16
  4.1 1.3 %collective-permute-start.1 = (f32[1,64,512]{2,1,0:T(8,128)S(1)}, f32[1,64,512]{2,1,0:T(8,128)S(1)}, u32[]{:S(2)}, u32[]{:S(2)}) collective-permute-start(f32[1,64,512]{2,1,0:T(8,128)S(1)} %get-tuple-element.19), channel_id=1, source_target_pairs={{2,0},{4,2},{6,4},{8,6},{10,8},{12,10},{14,12},{16,14},{18,16},{20... | collective-permute-start | bytes 393224 | tf_op jit(solution)/shard_map/ppermute | solution.py:17
  5.4 0.9 %slice_bitcast_fusion.7 = f32[1,4,1,512]{3,2,1,0:T(1,128)S(1)} fusion(f32[4,64,512]{2,1,0:T(8,128)} %param.10), kind=kLoop, calls=%fused_computation.59 | loop fusion | bytes 16384 | tf_op jit(solution)/shard_map/stack | solution.py:42
  6.3 4.2 %collective-permute-start.3 = (f32[2,4,1,512]{3,2,1,0:T(1,128)S(1)}, f32[2,4,1,512]{3,2,1,0:T(1,128)S(1)}, u32[]{:S(2)}, u32[]{:S(2)}) collective-permute-start(f32[2,4,1,512]{3,2,1,0:T(1,128)S(1)} %pad_maximum_fusion.3), channel_id=1, source_target_pairs={{0,1},{2,3},{4,5},{6,7},{8,9},{10,11},{12,13},{14,15},{16,17},{18,... | collective-permute-start | bytes 49160 | tf_op jit(solution)/shard_map/ppermute | solution.py:25
  10.5 0.9 %slice_bitcast_fusion.3 = f32[1,1,64,512]{3,2,1,0:T(8,128)S(1)} fusion(f32[4,64,512]{2,1,0:T(8,128)} %param.9), kind=kLoop, calls=%fused_computation.49 | loop fusion | bytes 262144 | tf_op jit(solution)/shard_map/stack | solution.py:41
  11.5 0.0 copy-start
  11.5 4.2 %collective-permute-start = (f32[2,1,64,512]{3,2,1,0:T(8,128)S(1)}, f32[2,1,64,512]{3,2,1,0:T(8,128)S(1)}, u32[]{:S(2)}, u32[]{:S(2)}) collective-permute-start(f32[2,1,64,512]{3,2,1,0:T(8,128)S(1)} %pad_maximum_fusion.2), channel_id=1, source_target_pairs={{0,2},{2,4},{4,6},{6,8},{8,10},{10,12},{12,14},{14,16},{16,18},{18... | collective-permute-start | bytes 786440 | tf_op jit(solution)/shard_map/ppermute | solution.py:25
  15.8 0.1 constant_dynamic-update-slice_fusion
  15.9 1.6 %collective-permute-start.5 = (f32[6,1,512]{2,1,0:T(1,128)S(1)}, f32[6,1,512]{2,1,0:T(1,128)S(1)}, u32[]{:S(2)}, u32[]{:S(2)}) collective-permute-start(f32[6,1,512]{2,1,0:T(1,128)S(1)} %get-tuple-element.15), channel_id=1, source_target_pairs={{0,1},{2,3},{4,5},{6,7},{8,9},{10,11},{12,13},{14,15},{16,17},{18,... | collective-permute-start | bytes 36872 | tf_op jit(solution)/shard_map/ppermute | solution.py:16
  17.5 0.0 copy-start.3
  17.5 1.4 %collective-permute-start.4 = (f32[6,1,512]{2,1,0:T(1,128)S(1)}, f32[6,1,512]{2,1,0:T(1,128)S(1)}, u32[]{:S(2)}, u32[]{:S(2)}) collective-permute-start(f32[6,1,512]{2,1,0:T(1,128)S(1)} %get-tuple-element.14), channel_id=1, source_target_pairs={{1,0},{3,2},{5,4},{7,6},{9,8},{11,10},{13,12},{15,14},{17,16},{19,... | collective-permute-start | bytes 36872 | tf_op jit(solution)/shard_map/ppermute | solution.py:17
  19.0 0.1 pad_maximum_fusion
  19.1 4.2 %collective-permute-done.4 = f32[6,1,512]{2,1,0:T(1,128)S(1)} collective-permute-done((f32[6,1,512]{2,1,0:T(1,128)S(1)}, f32[6,1,512]{2,1,0:T(1,128)S(1)}, u32[]{:S(2)}, u32[]{:S(2)}) %collective-permute-start.4) | collective-permute-done | bytes 12320 | tf_op jit(solution)/shard_map/ppermute | solution.py:17
  23.3 0.5 fusion.11
  23.8 0.1 slice_multiply_fusion
  23.9 0.0 copy-start.2
  23.9 1.0 %copy-done.2 = f32[4,64,512]{2,1,0:T(8,128)S(1)} copy-done((f32[4,64,512]{2,1,0:T(8,128)S(1)}, f32[4,64,512]{2,1,0:T(8,128)}, u32[]{:S(2)}) %copy-start.2) | copy-done | bytes 524312
  24.9 0.5 fusion.5
  25.4 0.1 slice_multiply_fusion.1
  25.5 0.9 %copy-done.4 = f32[4,64,512]{2,1,0:T(8,128)S(1)} copy-done((f32[4,64,512]{2,1,0:T(8,128)S(1)}, f32[4,64,512]{2,1,0:T(8,128)}, u32[]{:S(2)}) %copy-start.4) | copy-done | bytes 524312
  26.5 1.3 %multiply_reduce_fusion = (f32[]{:T(128)}, f32[]{:T(128)}, f32[]{:T(128)}, f32[]{:T(128)}, f32[4,64,512]{2,1,0:T(8,128)S(1)}) fusion(f32[4,64,512]{2,1,0:T(8,128)S(1)} %copy-done.4, f32[4,64,512]{2,1,0:T(8,128)S(1)} %copy-done, f32[4,64,512]{2,1,0:T(8,128)S(1)} %slice_multiply_fusion, f32[4,65,512]{2,1,0:T(8,128)S(1)} %fusion.11, ...), kind=kLoop, calls=%fused_computation.37 | loop fusion | flops 2490364 | bytes 4718608 | tf_op jit(solution)/shard_map/reduce_sum | solution.py:75
  27.8 40.8 %all-reduce.4 = (f32[]{:T(128)}, f32[]{:T(128)}, f32[]{:T(128)}, f32[]{:T(128)}) all-reduce(f32[]{:T(128)} %get-tuple-element.5, f32[]{:T(128)} %get-tuple-element.6, f32[]{:T(128)} %get-tuple-element.4, f32[]{:T(128)} %get-tuple-element.3), channel_id=1, replica_groups=mesh['il'=16,'xl'=2] {'il','xl'}, use_global_device_ids=true, to_apply=%region_1.2 | all-reduce | flops 4 | bytes 32 | tf_op jit(solution)/shard_map/psum | solution.py:70
  72.5 1.4 %multiply_add_fusion = (f32[4,64,512]{2,1,0:T(8,128)}, f32[4,64,512]{2,1,0:T(8,128)}, f32[4,64,512]{2,1,0:T(8,128)}) fusion(f32[4,64,512]{2,1,0:T(8,128)S(1)} %copy-done, f32[]{:T(128)S(6)} %div.7, f32[4,64,512]{2,1,0:T(8,128)S(1)} %copy-done.4, f32[4,64,512]{2,1,0:T(8,128)S(1)} %get-tuple-element.13, f32[]{:T(128)S(6)} %div.6, f32[4,64,512]{2,1,0:T(8,128)S(1)} %copy-done.5), kind=kLoop, calls=%fused_computation.36 | loop fusion | flops 786432 | bytes 3670024 | tf_op jit(solution)/shard_map/add | solution.py:83
  (23 shorter events, 0.2 us)
Async XLA Ops:
  0.6 4.8 %copy-start.1 = (f32[4,64,512]{2,1,0:T(8,128)S(1)}, f32[4,64,512]{2,1,0:T(8,128)}, u32[]{:S(2)}) copy-start(f32[4,64,512]{2,1,0:T(8,128)} %param.11) | copy-start | bytes 1572868
  1.7 14.1 %collective-permute-start.2 = (f32[1,64,512]{2,1,0:T(8,128)S(1)}, f32[1,64,512]{2,1,0:T(8,128)S(1)}, u32[]{:S(2)}, u32[]{:S(2)}) collective-permute-start(f32[1,64,512]{2,1,0:T(8,128)S(1)} %get-tuple-element.20), channel_id=1, source_target_pairs={{0,2},{2,4},{4,6},{6,8},{8,10},{10,12},{12,14},{14,16},{16,18},{18... | collective-permute-start | bytes 393224 | tf_op jit(solution)/shard_map/ppermute | solution.py:16
  4.1 11.8 %collective-permute-start.1 = (f32[1,64,512]{2,1,0:T(8,128)S(1)}, f32[1,64,512]{2,1,0:T(8,128)S(1)}, u32[]{:S(2)}, u32[]{:S(2)}) collective-permute-start(f32[1,64,512]{2,1,0:T(8,128)S(1)} %get-tuple-element.19), channel_id=1, source_target_pairs={{2,0},{4,2},{6,4},{8,6},{10,8},{12,10},{14,12},{16,14},{18,16},{20... | collective-permute-start | bytes 393224 | tf_op jit(solution)/shard_map/ppermute | solution.py:17
  6.3 11.2 %collective-permute-start.3 = (f32[2,4,1,512]{3,2,1,0:T(1,128)S(1)}, f32[2,4,1,512]{3,2,1,0:T(1,128)S(1)}, u32[]{:S(2)}, u32[]{:S(2)}) collective-permute-start(f32[2,4,1,512]{3,2,1,0:T(1,128)S(1)} %pad_maximum_fusion.3), channel_id=1, source_target_pairs={{0,1},{2,3},{4,5},{6,7},{8,9},{10,11},{12,13},{14,15},{16,17},{18,... | collective-permute-start | bytes 49160 | tf_op jit(solution)/shard_map/ppermute | solution.py:25
  11.5 4.3 %copy-start = (f32[4,64,512]{2,1,0:T(8,128)S(1)}, f32[4,64,512]{2,1,0:T(8,128)}, u32[]{:S(2)}) copy-start(f32[4,64,512]{2,1,0:T(8,128)} %param.8) | copy-start | bytes 1572868
  11.5 12.4 %collective-permute-start = (f32[2,1,64,512]{3,2,1,0:T(8,128)S(1)}, f32[2,1,64,512]{3,2,1,0:T(8,128)S(1)}, u32[]{:S(2)}, u32[]{:S(2)}) collective-permute-start(f32[2,1,64,512]{3,2,1,0:T(8,128)S(1)} %pad_maximum_fusion.2), channel_id=1, source_target_pairs={{0,2},{2,4},{4,6},{6,8},{8,10},{10,12},{12,14},{14,16},{16,18},{18... | collective-permute-start | bytes 786440 | tf_op jit(solution)/shard_map/ppermute | solution.py:25
  15.9 3.0 %collective-permute-start.5 = (f32[6,1,512]{2,1,0:T(1,128)S(1)}, f32[6,1,512]{2,1,0:T(1,128)S(1)}, u32[]{:S(2)}, u32[]{:S(2)}) collective-permute-start(f32[6,1,512]{2,1,0:T(1,128)S(1)} %get-tuple-element.15), channel_id=1, source_target_pairs={{0,1},{2,3},{4,5},{6,7},{8,9},{10,11},{12,13},{14,15},{16,17},{18,... | collective-permute-start | bytes 36872 | tf_op jit(solution)/shard_map/ppermute | solution.py:16
  17.5 5.7 %copy-start.3 = (f32[4,64,512]{2,1,0:T(8,128)S(1)}, f32[4,64,512]{2,1,0:T(8,128)}, u32[]{:S(2)}) copy-start(f32[4,64,512]{2,1,0:T(8,128)} %param.10) | copy-start | bytes 1572868
  17.5 5.7 %collective-permute-start.4 = (f32[6,1,512]{2,1,0:T(1,128)S(1)}, f32[6,1,512]{2,1,0:T(1,128)S(1)}, u32[]{:S(2)}, u32[]{:S(2)}) collective-permute-start(f32[6,1,512]{2,1,0:T(1,128)S(1)} %get-tuple-element.14), channel_id=1, source_target_pairs={{1,0},{3,2},{5,4},{7,6},{9,8},{11,10},{13,12},{15,14},{17,16},{19,... | collective-permute-start | bytes 36872 | tf_op jit(solution)/shard_map/ppermute | solution.py:17
  23.9 1.0 %copy-start.2 = (f32[4,64,512]{2,1,0:T(8,128)S(1)}, f32[4,64,512]{2,1,0:T(8,128)}, u32[]{:S(2)}) copy-start(f32[4,64,512]{2,1,0:T(8,128)} %param.9) | copy-start | bytes 1572868
  25.4 1.0 %copy-start.4 = (f32[4,64,512]{2,1,0:T(8,128)S(1)}, f32[4,64,512]{2,1,0:T(8,128)}, u32[]{:S(2)}) copy-start(f32[4,64,512]{2,1,0:T(8,128)} %param.7) | copy-start | bytes 1572868
  26.5 46.0 %copy-start.5 = (f32[4,64,512]{2,1,0:T(8,128)S(1)}, f32[4,64,512]{2,1,0:T(8,128)}, u32[]{:S(2)}) copy-start(f32[4,64,512]{2,1,0:T(8,128)} %param.6) | copy-start | bytes 1572868
where the time goes:
time: 74.4 us; the launch traced here: 73.8 us
  blocking collectives  40.8 us (55%)
  starting transfers between devices  15.1 us (20%)
  local copies, waits for them, and re-layouts  4.96 us (7%)
  between operations  4.8 us (6%)
  waiting for transfers between devices  4.21 us (6%)
  other arithmetic  3.96 us (5%)
    psum x1, blocking collectives, body(): lax.psum((jnp.sum(residual * residual), jnp.sum(direction * image), jnp.s...  40.8 us
    ppermute x2, starting transfers between devices, shifted(): return lax.ppermute(value, axis, pairs)  8.41 us
    ppermute x2, waiting for transfers between devices, padded_2(): after = lax.ppermute(first, axis, down)  4.2 us
    ppermute x2, starting transfers between devices, padded_2(): before = lax.ppermute(last, axis, up)  3.98 us
    ppermute x2, starting transfers between devices, padded_2(): after = lax.ppermute(first, axis, down)  2.72 us
    unnamed x13, local copies, waits for them, and re-layouts  1.99 us
  transfers between devices with their start and end apart: 6, of which 1 were waited for; matrix products, arithmetic and copies ran while one was open for 4% of the time, Pallas kernels for 0%

commit v1 on v0

--- a/solution.py
+++ b/solution.py
@@ -68,13 +68,16 @@
 def body(solution, residual, direction, slope_il, slope_xl, weights):
     image = normal_apply(direction, slope_il, slope_xl, weights)
     norm_old, along, cross_term, image_norm = lax.psum(
-        (
-            jnp.sum(residual * residual),
-            jnp.sum(direction * image),
-            jnp.sum(residual * image),
-            jnp.sum(image * image),
+        lax.psum(
+            (
+                jnp.sum(residual * residual),
+                jnp.sum(direction * image),
+                jnp.sum(residual * image),
+                jnp.sum(image * image),
+            ),
+            "xl",
         ),
-        ("il", "xl"),
+        "il",
     )
     alpha = norm_old / along
     new_residual = residual - alpha * image

time: 74.4 us -> 69.2 us (0.930)
  blocking collectives: 40.8 us -> 35.8 us
    psum x1, blocking collectives: 40.8 us -> 5.56 us  [body(): lax.psum((jnp.sum(residual * residual), jnp.sum(direction * image), jnp.s...]
    psum x0 -> x1, blocking collectives: none -> 30.2 us  [body(): lax.psum(lax.psum((jnp.sum(residual * residual), jnp.sum(direction * imag...]
where the time goes in v1:
time: 69.2 us; the launch traced here: 68.7 us
  blocking collectives  35.8 us (52%)
  starting transfers between devices  15.1 us (22%)
  local copies, waits for them, and re-layouts  4.96 us (7%)
  between operations  4.79 us (7%)
  waiting for transfers between devices  4.21 us (6%)
  other arithmetic  3.88 us (6%)
    psum x1, blocking collectives, body(): lax.psum(lax.psum((jnp.sum(residual * residual), jnp.sum(direction * imag...  30.2 us
    ppermute x2, starting transfers between devices, shifted(): return lax.ppermute(value, axis, pairs)  8.41 us
    psum x1, blocking collectives, body(): lax.psum((jnp.sum(residual * residual), jnp.sum(direction * image), jnp.s...  5.56 us
    ppermute x2, waiting for transfers between devices, padded_2(): after = lax.ppermute(first, axis, down)  4.2 us
    ppermute x2, starting transfers between devices, padded_2(): before = lax.ppermute(last, axis, up)  3.98 us
    ppermute x2, starting transfers between devices, padded_2(): after = lax.ppermute(first, axis, down)  2.72 us
    unnamed x13, local copies, waits for them, and re-layouts  1.99 us
  transfers between devices with their start and end apart: 6, of which 1 were waited for; matrix products, arithmetic and copies ran while one was open for 4% of the time, Pallas kernels for 0%

profile of v1, /device:TPU:0, one launch (start us, length us, event | category | flops | bytes accessed | tf_op | source)
XLA Modules:
  0.0 68.7 jit_solution(1682389726481165762)
XLA Ops:
  0.6 1.0 %fusion.23 = (f32[1,64,512]{2,1,0:T(8,128)S(1)}, f32[1,64,512]{2,1,0:T(8,128)S(1)}) fusion(f32[4,64,512]{2,1,0:T(8,128)} %param.8), kind=kLoop, calls=%fused_computation.63 | loop fusion | bytes 524288 | tf_op jit(solution)/shard_map/slice | solution.py:15
  1.7 2.4 %collective-permute-start.2 = (f32[1,64,512]{2,1,0:T(8,128)S(1)}, f32[1,64,512]{2,1,0:T(8,128)S(1)}, u32[]{:S(2)}, u32[]{:S(2)}) collective-permute-start(f32[1,64,512]{2,1,0:T(8,128)S(1)} %get-tuple-element.24), channel_id=1, source_target_pairs={{0,2},{2,4},{4,6},{6,8},{8,10},{10,12},{12,14},{14,16},{16,18},{18... | collective-permute-start | bytes 393224 | tf_op jit(solution)/shard_map/ppermute | solution.py:16
  4.1 1.3 %collective-permute-start.1 = (f32[1,64,512]{2,1,0:T(8,128)S(1)}, f32[1,64,512]{2,1,0:T(8,128)S(1)}, u32[]{:S(2)}, u32[]{:S(2)}) collective-permute-start(f32[1,64,512]{2,1,0:T(8,128)S(1)} %get-tuple-element.23), channel_id=1, source_target_pairs={{2,0},{4,2},{6,4},{8,6},{10,8},{12,10},{14,12},{16,14},{18,16},{20... | collective-permute-start | bytes 393224 | tf_op jit(solution)/shard_map/ppermute | solution.py:17
  5.4 0.9 %slice_bitcast_fusion.7 = f32[1,4,1,512]{3,2,1,0:T(1,128)S(1)} fusion(f32[4,64,512]{2,1,0:T(8,128)} %param.10), kind=kLoop, calls=%fused_computation.59 | loop fusion | bytes 16384 | tf_op jit(solution)/shard_map/stack | solution.py:42
  6.3 4.2 %collective-permute-start.3 = (f32[2,4,1,512]{3,2,1,0:T(1,128)S(1)}, f32[2,4,1,512]{3,2,1,0:T(1,128)S(1)}, u32[]{:S(2)}, u32[]{:S(2)}) collective-permute-start(f32[2,4,1,512]{3,2,1,0:T(1,128)S(1)} %pad_maximum_fusion.3), channel_id=1, source_target_pairs={{0,1},{2,3},{4,5},{6,7},{8,9},{10,11},{12,13},{14,15},{16,17},{18,... | collective-permute-start | bytes 49160 | tf_op jit(solution)/shard_map/ppermute | solution.py:25
  10.5 0.9 %slice_bitcast_fusion.3 = f32[1,1,64,512]{3,2,1,0:T(8,128)S(1)} fusion(f32[4,64,512]{2,1,0:T(8,128)} %param.9), kind=kLoop, calls=%fused_computation.49 | loop fusion | bytes 262144 | tf_op jit(solution)/shard_map/stack | solution.py:41
  11.5 0.0 copy-start
  11.5 4.2 %collective-permute-start = (f32[2,1,64,512]{3,2,1,0:T(8,128)S(1)}, f32[2,1,64,512]{3,2,1,0:T(8,128)S(1)}, u32[]{:S(2)}, u32[]{:S(2)}) collective-permute-start(f32[2,1,64,512]{3,2,1,0:T(8,128)S(1)} %pad_maximum_fusion.2), channel_id=1, source_target_pairs={{0,2},{2,4},{4,6},{6,8},{8,10},{10,12},{12,14},{14,16},{16,18},{18... | collective-permute-start | bytes 786440 | tf_op jit(solution)/shard_map/ppermute | solution.py:25
  15.8 0.1 constant_dynamic-update-slice_fusion
  15.9 1.6 %collective-permute-start.5 = (f32[6,1,512]{2,1,0:T(1,128)S(1)}, f32[6,1,512]{2,1,0:T(1,128)S(1)}, u32[]{:S(2)}, u32[]{:S(2)}) collective-permute-start(f32[6,1,512]{2,1,0:T(1,128)S(1)} %get-tuple-element.19), channel_id=1, source_target_pairs={{0,1},{2,3},{4,5},{6,7},{8,9},{10,11},{12,13},{14,15},{16,17},{18,... | collective-permute-start | bytes 36872 | tf_op jit(solution)/shard_map/ppermute | solution.py:16
  17.5 1.4 %collective-permute-start.4 = (f32[6,1,512]{2,1,0:T(1,128)S(1)}, f32[6,1,512]{2,1,0:T(1,128)S(1)}, u32[]{:S(2)}, u32[]{:S(2)}) collective-permute-start(f32[6,1,512]{2,1,0:T(1,128)S(1)} %get-tuple-element.18), channel_id=1, source_target_pairs={{1,0},{3,2},{5,4},{7,6},{9,8},{11,10},{13,12},{15,14},{17,16},{19,... | collective-permute-start | bytes 36872 | tf_op jit(solution)/shard_map/ppermute | solution.py:17
  19.0 0.1 pad_maximum_fusion
  19.1 4.2 %collective-permute-done.4 = f32[6,1,512]{2,1,0:T(1,128)S(1)} collective-permute-done((f32[6,1,512]{2,1,0:T(1,128)S(1)}, f32[6,1,512]{2,1,0:T(1,128)S(1)}, u32[]{:S(2)}, u32[]{:S(2)}) %collective-permute-start.4) | collective-permute-done | bytes 12320 | tf_op jit(solution)/shard_map/ppermute | solution.py:17
  23.3 0.5 fusion.11
  23.8 0.1 slice_multiply_fusion
  23.9 0.0 copy-start.2
  23.9 1.0 %copy-done.2 = f32[4,64,512]{2,1,0:T(8,128)S(1)} copy-done((f32[4,64,512]{2,1,0:T(8,128)S(1)}, f32[4,64,512]{2,1,0:T(8,128)}, u32[]{:S(2)}) %copy-start.2) | copy-done | bytes 524312
  24.9 0.5 fusion.5
  25.4 0.1 slice_multiply_fusion.1
  25.5 0.9 %copy-done.4 = f32[4,64,512]{2,1,0:T(8,128)S(1)} copy-done((f32[4,64,512]{2,1,0:T(8,128)S(1)}, f32[4,64,512]{2,1,0:T(8,128)}, u32[]{:S(2)}) %copy-start.4) | copy-done | bytes 524312
  26.5 1.2 %multiply_reduce_fusion = (f32[]{:T(128)}, f32[]{:T(128)}, f32[]{:T(128)}, f32[]{:T(128)}, f32[4,64,512]{2,1,0:T(8,128)S(1)}) fusion(f32[4,64,512]{2,1,0:T(8,128)S(1)} %copy-done.4, f32[4,64,512]{2,1,0:T(8,128)S(1)} %copy-done, f32[4,64,512]{2,1,0:T(8,128)S(1)} %slice_multiply_fusion, f32[4,65,512]{2,1,0:T(8,128)S(1)} %fusion.11, ...), kind=kLoop, calls=%fused_computation.37 | loop fusion | flops 2490364 | bytes 4718608 | tf_op jit(solution)/shard_map/reduce_sum | solution.py:76
  27.7 5.6 %all-reduce.5 = (f32[]{:T(128)}, f32[]{:T(128)}, f32[]{:T(128)}, f32[]{:T(128)}) all-reduce(f32[]{:T(128)} %get-tuple-element.5, f32[]{:T(128)} %get-tuple-element.6, f32[]{:T(128)} %get-tuple-element.4, f32[]{:T(128)} %get-tuple-element.3), channel_id=1, replica_groups=mesh['il'=16,'xl'=2] {'xl'}, use_global_device_ids=true, to_apply=%region_1.2 | all-reduce | flops 4 | bytes 32 | tf_op jit(solution)/shard_map/psum | solution.py:71
  33.3 30.2 %all-reduce.4 = (f32[]{:T(128)}, f32[]{:T(128)}, f32[]{:T(128)}, f32[]{:T(128)}) all-reduce(f32[]{:T(128)} %get-tuple-element.11, f32[]{:T(128)} %get-tuple-element.12, f32[]{:T(128)} %get-tuple-element.13, f32[]{:T(128)} %get-tuple-element.14), channel_id=1, replica_groups=mesh['il'=16,'xl'=2] {'il'}, use_global_device_ids=true, to_apply=%region_2.3 | all-reduce | flops 4 | bytes 32 | tf_op jit(solution)/shard_map/psum | solution.py:70
  67.4 1.4 %multiply_add_fusion = (f32[4,64,512]{2,1,0:T(8,128)}, f32[4,64,512]{2,1,0:T(8,128)}, f32[4,64,512]{2,1,0:T(8,128)}) fusion(f32[4,64,512]{2,1,0:T(8,128)S(1)} %copy-done, f32[]{:T(128)S(6)} %div.7, f32[4,64,512]{2,1,0:T(8,128)S(1)} %copy-done.4, f32[4,64,512]{2,1,0:T(8,128)S(1)} %get-tuple-element.17, f32[]{:T(128)S(6)} %div.6, f32[4,64,512]{2,1,0:T(8,128)S(1)} %copy-done.5), kind=kLoop, calls=%fused_computation.36 | loop fusion | flops 786432 | bytes 3670024 | tf_op jit(solution)/shard_map/add | solution.py:86
  (24 shorter events, 0.2 us)
Async XLA Ops:
  0.6 4.8 %copy-start.1 = (f32[4,64,512]{2,1,0:T(8,128)S(1)}, f32[4,64,512]{2,1,0:T(8,128)}, u32[]{:S(2)}) copy-start(f32[4,64,512]{2,1,0:T(8,128)} %param.11) | copy-start | bytes 1572868
  1.7 14.1 %collective-permute-start.2 = (f32[1,64,512]{2,1,0:T(8,128)S(1)}, f32[1,64,512]{2,1,0:T(8,128)S(1)}, u32[]{:S(2)}, u32[]{:S(2)}) collective-permute-start(f32[1,64,512]{2,1,0:T(8,128)S(1)} %get-tuple-element.24), channel_id=1, source_target_pairs={{0,2},{2,4},{4,6},{6,8},{8,10},{10,12},{12,14},{14,16},{16,18},{18... | collective-permute-start | bytes 393224 | tf_op jit(solution)/shard_map/ppermute | solution.py:16
  4.1 11.8 %collective-permute-start.1 = (f32[1,64,512]{2,1,0:T(8,128)S(1)}, f32[1,64,512]{2,1,0:T(8,128)S(1)}, u32[]{:S(2)}, u32[]{:S(2)}) collective-permute-start(f32[1,64,512]{2,1,0:T(8,128)S(1)} %get-tuple-element.23), channel_id=1, source_target_pairs={{2,0},{4,2},{6,4},{8,6},{10,8},{12,10},{14,12},{16,14},{18,16},{20... | collective-permute-start | bytes 393224 | tf_op jit(solution)/shard_map/ppermute | solution.py:17
  6.3 11.2 %collective-permute-start.3 = (f32[2,4,1,512]{3,2,1,0:T(1,128)S(1)}, f32[2,4,1,512]{3,2,1,0:T(1,128)S(1)}, u32[]{:S(2)}, u32[]{:S(2)}) collective-permute-start(f32[2,4,1,512]{3,2,1,0:T(1,128)S(1)} %pad_maximum_fusion.3), channel_id=1, source_target_pairs={{0,1},{2,3},{4,5},{6,7},{8,9},{10,11},{12,13},{14,15},{16,17},{18,... | collective-permute-start | bytes 49160 | tf_op jit(solution)/shard_map/ppermute | solution.py:25
  11.5 4.3 %copy-start = (f32[4,64,512]{2,1,0:T(8,128)S(1)}, f32[4,64,512]{2,1,0:T(8,128)}, u32[]{:S(2)}) copy-start(f32[4,64,512]{2,1,0:T(8,128)} %param.8) | copy-start | bytes 1572868
  11.5 12.4 %collective-permute-start = (f32[2,1,64,512]{3,2,1,0:T(8,128)S(1)}, f32[2,1,64,512]{3,2,1,0:T(8,128)S(1)}, u32[]{:S(2)}, u32[]{:S(2)}) collective-permute-start(f32[2,1,64,512]{3,2,1,0:T(8,128)S(1)} %pad_maximum_fusion.2), channel_id=1, source_target_pairs={{0,2},{2,4},{4,6},{6,8},{8,10},{10,12},{12,14},{14,16},{16,18},{18... | collective-permute-start | bytes 786440 | tf_op jit(solution)/shard_map/ppermute | solution.py:25
  15.9 3.0 %collective-permute-start.5 = (f32[6,1,512]{2,1,0:T(1,128)S(1)}, f32[6,1,512]{2,1,0:T(1,128)S(1)}, u32[]{:S(2)}, u32[]{:S(2)}) collective-permute-start(f32[6,1,512]{2,1,0:T(1,128)S(1)} %get-tuple-element.19), channel_id=1, source_target_pairs={{0,1},{2,3},{4,5},{6,7},{8,9},{10,11},{12,13},{14,15},{16,17},{18,... | collective-permute-start | bytes 36872 | tf_op jit(solution)/shard_map/ppermute | solution.py:16
  17.5 5.7 %copy-start.3 = (f32[4,64,512]{2,1,0:T(8,128)S(1)}, f32[4,64,512]{2,1,0:T(8,128)}, u32[]{:S(2)}) copy-start(f32[4,64,512]{2,1,0:T(8,128)} %param.10) | copy-start | bytes 1572868
  17.5 5.7 %collective-permute-start.4 = (f32[6,1,512]{2,1,0:T(1,128)S(1)}, f32[6,1,512]{2,1,0:T(1,128)S(1)}, u32[]{:S(2)}, u32[]{:S(2)}) collective-permute-start(f32[6,1,512]{2,1,0:T(1,128)S(1)} %get-tuple-element.18), channel_id=1, source_target_pairs={{1,0},{3,2},{5,4},{7,6},{9,8},{11,10},{13,12},{15,14},{17,16},{19,... | collective-permute-start | bytes 36872 | tf_op jit(solution)/shard_map/ppermute | solution.py:17
  23.9 1.0 %copy-start.2 = (f32[4,64,512]{2,1,0:T(8,128)S(1)}, f32[4,64,512]{2,1,0:T(8,128)}, u32[]{:S(2)}) copy-start(f32[4,64,512]{2,1,0:T(8,128)} %param.9) | copy-start | bytes 1572868
  25.4 1.0 %copy-start.4 = (f32[4,64,512]{2,1,0:T(8,128)S(1)}, f32[4,64,512]{2,1,0:T(8,128)}, u32[]{:S(2)}) copy-start(f32[4,64,512]{2,1,0:T(8,128)} %param.7) | copy-start | bytes 1572868
  26.5 40.9 %copy-start.5 = (f32[4,64,512]{2,1,0:T(8,128)S(1)}, f32[4,64,512]{2,1,0:T(8,128)}, u32[]{:S(2)}) copy-start(f32[4,64,512]{2,1,0:T(8,128)} %param.6) | copy-start | bytes 1572868
